TPU v7x, 512 devices: a whole 4x4x16 slice. The times are simulated.
512 devices in a mesh: adapter: 32 (over z, core), tensor: 16 (over x, y).
Axes of the slice: x: 4, y: 4, z: 16, core: 2. Of those that a mesh axis runs over, the one named last changes fastest.
Arguments:
- attn_output: bfloat16 [8192, 8192], P('adapter', 'tensor'), may hold values from -6 to 6
- output_grad: bfloat16 [8192, 8192], P(('adapter', 'tensor')), may hold values from -6 to 6
- adapter_ids: int32 [8192], P('adapter'), may hold values from 0 to 1023, as said below
- base_weight: bfloat16 [8192, 8192], P('tensor', 'adapter'), may hold values from -0.0625 to 0.0625
- adapter_down: bfloat16 [8192, 16384], P('tensor', 'adapter'), may hold values from -0.1796875 to 0.1796875
- adapter_up: bfloat16 [16384, 8192], P('adapter', 'tensor'), may hold values from -0.0625 to 0.0625
Outputs:
- attention_output_gradient: bfloat16 [8192, 8192], P('adapter', 'tensor')
- down_grad: float32 [8192, 16384], P('tensor', 'adapter')
- up_grad: float32 [16384, 8192], P('adapter', 'tensor')
Inputs may be any that keep to these rules, and one draw needn't show every extreme that they name: `adapter_ids`: the 256 tokens of each index of adapter form one block; the owner of adapter a is a // 32. At most 20 tokens of a block have adapters of one owner, and one owner, drawn from the seed, gets exactly 20 tokens of every block.
All inputs are finite; a program needn't handle non-finite values.
Results may differ from a plain program's by a relative error of at most 0.007.
Values may be sent and summed in bfloat16 or wider, within the bound.
A program may use at most 64 MiB of HBM per device.

v0:
```python
import jax
import jax.numpy as jnp
from jax import lax
from jax.sharding import PartitionSpec as P

ADAPTER_RANK = 16


ADAPTER_SCALE = 2.0


def per_device(attn_output, output_grad, adapter_ids, base_weight, adapter_down, adapter_up):
    owners = lax.axis_size("adapter")
    tok_rows, width_part = attn_output.shape
    capacity = 5 * tok_rows // (2 * owners)
    adapter_slot_count = owners * capacity
    per_owner = adapter_down.shape[1] // ADAPTER_RANK
    full_grad = lax.all_gather(output_grad, "tensor", axis=0, tiled=True)
    start_col = lax.axis_index("tensor") * width_part
    grad_part = lax.dynamic_slice_in_dim(full_grad, start_col, width_part, 1)
    frozen_gradient = lax.dot_general(
        full_grad,
        lax.all_gather(base_weight, "adapter", axis=1, tiled=True),
        (((1,), (1,)), ((), ())),
        preferred_element_type=jnp.float32,
    )
    owner_of = adapter_ids // per_owner
    local_of = adapter_ids % per_owner
    onehot_own = (owner_of[:, None] == jnp.arange(owners, dtype=jnp.int32)[None, :]).astype(
        jnp.int32
    )
    before = jnp.cumsum(onehot_own, axis=0) - onehot_own
    rank_in = jnp.sum(before * onehot_own, axis=1)
    token_slot_index = owner_of * capacity + rank_in
    source_row = (
        jnp.full((adapter_slot_count,), tok_rows, jnp.int32)
        .at[token_slot_index]
        .set(jnp.arange(tok_rows, dtype=jnp.int32))
    )
    send_inputs = jnp.concatenate([attn_output, jnp.zeros((1, width_part), jnp.bfloat16)], axis=0)[
        source_row
    ]
    send_grads = jnp.concatenate([grad_part, jnp.zeros((1, width_part), jnp.bfloat16)], axis=0)[
        source_row
    ]
    send_labels = jnp.concatenate(
        [local_of.astype(jnp.bfloat16), jnp.full((1,), -1.0, jnp.bfloat16)]
    )[source_row]
    recv_inputs, recv_grads, recv_labels = (
        lax.all_to_all(send_inputs, "adapter", split_axis=0, concat_axis=0, tiled=True),
        lax.all_to_all(send_grads, "adapter", split_axis=0, concat_axis=0, tiled=True),
        lax.all_to_all(send_labels, "adapter", split_axis=0, concat_axis=0, tiled=True),
    )
    chosen = (
        recv_labels.astype(jnp.float32)[:, None]
        == jnp.arange(per_owner, dtype=jnp.float32)[None, :]
    ).astype(jnp.float32)
    spread = jnp.repeat(chosen, ADAPTER_RANK, axis=1)
    proj_inputs = jnp.dot(recv_inputs, adapter_down, preferred_element_type=jnp.float32)
    proj_grads = lax.dot_general(
        recv_grads, adapter_up, (((1,), (1,)), ((), ())), preferred_element_type=jnp.float32
    )
    rank_inputs = (
        (proj_inputs * spread)
        .reshape(adapter_slot_count, per_owner, ADAPTER_RANK)
        .sum(axis=1)
        .reshape(-1)
    )
    rank_gradients = (
        (proj_grads * spread)
        .reshape(adapter_slot_count, per_owner, ADAPTER_RANK)
        .sum(axis=1)
        .reshape(-1)
    )
    rank_inputs, rank_gradients = lax.psum((rank_inputs, rank_gradients), "tensor")
    scaled_up_weight = (
        ADAPTER_SCALE * rank_inputs.reshape(adapter_slot_count, ADAPTER_RANK)
    ).astype(jnp.bfloat16)
    rank_gradient = (
        ADAPTER_SCALE * rank_gradients.reshape(adapter_slot_count, ADAPTER_RANK)
    ).astype(jnp.bfloat16)
    spread_half = spread.astype(jnp.bfloat16)
    wide_gradient = jnp.tile(rank_gradient, (1, per_owner)) * spread_half
    up_wide = jnp.tile(scaled_up_weight, (1, per_owner)) * spread_half
    down_grad = lax.dot_general(
        recv_inputs, wide_gradient, (((0,), (0,)), ((), ())), preferred_element_type=jnp.float32
    )
    up_grad = lax.dot_general(
        up_wide, recv_grads, (((0,), (0,)), ((), ())), preferred_element_type=jnp.float32
    )
    adapter_block = lax.dot_general(
        wide_gradient, adapter_down, (((1,), (1,)), ((), ())), preferred_element_type=jnp.float32
    ).astype(jnp.bfloat16)
    returned_gradient = lax.all_to_all(
        adapter_block, "adapter", split_axis=0, concat_axis=0, tiled=True
    )
    adapter_contribution = returned_gradient[token_slot_index]
    attention_output_gradient = (frozen_gradient + adapter_contribution.astype(jnp.float32)).astype(
        jnp.bfloat16
    )
    return (attention_output_gradient, down_grad, up_grad)


def solution(mesh):
    placed = (
        P("adapter", "tensor"),
        P(("adapter", "tensor"), None),
        P("adapter"),
        P("tensor", "adapter"),
        P("tensor", "adapter"),
        P("adapter", "tensor"),
    )
    return jax.shard_map(
        per_device,
        mesh=mesh,
        in_specs=placed,
        out_specs=(P("adapter", "tensor"), P("tensor", "adapter"), P("adapter", "tensor")),
        check_vma=False,
    )
```

profile of v0, /device:TPU:1, one launch (start us, length us, event | category | flops | bytes accessed | tf_op | source)
XLA Modules:
  0.0 328.6 jit_solution(10062929042022065779)
XLA Ops:
  8.0 0.0 copy-start
  8.0 0.0 all-gather.3.cloned.1.call-start
  8.1 0.7 all-gather.3.cloned.1.call-update
  8.7 0.7 and_select_fusion.1
  9.4 0.6 reduce-window.6
  10.0 0.2 slice_reduce_fusion
  10.3 0.1 fusion.5
  10.4 1.4 scatter_custom_fusion
  11.8 4.3 %gather_fusion.1 = bf16[640]{0:T(1024)(128)(2,1)S(1)} fusion(bf16[257]{0:T(512)(128)(2,1)S(1)} %pad_maximum_fusion, s32[1024]{0:T(1024)S(1)} %pad_clamp_fusion.1), kind=kCustom, calls=%fused_computation.1 | custom fusion | bytes 5120 | tf_op jit(solution)/shard_map/gather | solution.py:46
  16.2 0.7 all_to_all.41
  16.9 16.7 %all-to-all-start.1 = ((bf16[32,20,1]{1,2,0:T(2,128)(2,1)}), bf16[32,20,1]{1,2,0:T(2,128)(2,1)S(1)}, u32[]{:S(2)}, u32[]{:S(2)}) async-start(bf16[32,20,1]{1,2,0:T(2,128)(2,1)} %all_to_all.41), calls=%async_computation.1 | async-start | bytes 32768 | tf_op jit(solution)/shard_map/all_to_all | solution.py:52
  33.6 1.0 concatenate.11
  34.6 2.8 gather_fusion.3
  37.4 1.0 all_to_all.38
  38.4 7.0 %all-to-all-done.1 = bf16[32,20,1]{1,2,0:T(2,128)(2,1)S(1)} async-done(((bf16[32,20,1]{1,2,0:T(2,128)(2,1)}), bf16[32,20,1]{1,2,0:T(2,128)(2,1)S(1)}, u32[]{:S(2)}, u32[]{:S(2)}) %all-to-all-start.1) | async-done | bytes 1312 | tf_op jit(solution)/shard_map/all_to_all | solution.py:52
  45.4 5.2 %all-to-all-start.3 = ((bf16[32,20,512]{2,1,0:T(8,128)(2,1)}), bf16[32,20,512]{2,1,0:T(8,128)(2,1)S(1)}, u32[]{:S(2)}, u32[]{:S(2)}) async-start(bf16[32,20,512]{2,1,0:T(8,128)(2,1)} %all_to_all.38), calls=%async_computation.3 | async-start | bytes 1572864 | tf_op jit(solution)/shard_map/all_to_all | solution.py:50
  50.6 33.1 %all-gather.3.cloned.1.call-done = bf16[256,8192]{1,0:T(8,128)(2,1)} async-done(((bf16[16,8192]{1,0:T(8,128)(2,1)}), bf16[256,8192]{1,0:T(8,128)(2,1)}) %all-gather.3.cloned.1.call-update) | async-done | bytes 4194320 | tf_op jit(solution)/shard_map/all_gather | solution.py:18
  83.7 1.0 constant_dynamic-slice_fusion
  84.7 2.8 gather_fusion
  87.5 1.0 all_to_all.30
  88.5 6.7 %all-to-all-done.3 = bf16[32,20,512]{2,1,0:T(8,128)(2,1)S(1)} async-done(((bf16[32,20,512]{2,1,0:T(8,128)(2,1)}), bf16[32,20,512]{2,1,0:T(8,128)(2,1)S(1)}, u32[]{:S(2)}, u32[]{:S(2)}) %all-to-all-start.3) | async-done | bytes 655392 | tf_op jit(solution)/shard_map/all_to_all | solution.py:50
  95.2 6.5 %all-to-all-start = ((bf16[32,20,512]{2,1,0:T(8,128)(2,1)}), bf16[32,20,512]{2,1,0:T(8,128)(2,1)S(1)}, u32[]{:S(2)}, u32[]{:S(2)}) async-start(bf16[32,20,512]{2,1,0:T(8,128)(2,1)} %all_to_all.30), calls=%async_computation | async-start | bytes 1572864 | tf_op jit(solution)/shard_map/all_to_all | solution.py:51
  101.7 0.0 all-reduce.5.cloned.1.call-start
  101.8 0.1 convert_reduce_fusion
  101.8 0.1 reshape.108
  101.9 0.1 all_to_all.40
  102.1 0.0 copy-done
  102.1 0.6 bitcast_multiply_fusion
  102.7 0.1 reduce_sum.29
  102.8 0.2 copy.16
  103.0 0.8 reshape.107
  103.7 42.6 %all-to-all-done = bf16[32,20,512]{2,1,0:T(8,128)(2,1)S(1)} async-done(((bf16[32,20,512]{2,1,0:T(8,128)(2,1)}), bf16[32,20,512]{2,1,0:T(8,128)(2,1)S(1)}, u32[]{:S(2)}, u32[]{:S(2)}) %all-to-all-start) | async-done | bytes 655392 | tf_op jit(solution)/shard_map/all_to_all | solution.py:51
  146.3 0.1 all_to_all.32
  146.5 1.6 bitcast_multiply_fusion.1
  148.1 0.1 reduce_sum.28
  148.2 0.2 copy.14
  148.4 0.8 reshape.105
  149.1 0.0 all-reduce.5.cloned.1.call-update
  149.1 0.0 all-gather.5.cloned.1.call-start
  149.2 0.5 all-gather.5.cloned.1.call-update
  149.7 100.1 %all-reduce.5.cloned.1.call-done = (f32[10240]{0:T(1024)}, f32[10240]{0:T(1024)}) async-done(((f32[10240]{0:T(1024)}, f32[10240]{0:T(1024)}), (f32[10240]{0:T(1024)}, f32[10240]{0:T(1024)})) %all-reduce.5.cloned.1.call-update) | async-done | bytes 81936 | tf_op jit(solution)/shard_map/psum | solution.py:75
  249.8 0.8 multiply_convert_fusion
  250.6 0.1 convert_element_type.68
  250.7 0.1 copy.15
  250.8 0.1 fusion.1
  251.0 0.6 convolution_convert_fusion
  251.5 1.1 all_to_all.35
  252.6 14.9 %all-to-all-start.2 = ((bf16[32,20,512]{2,1,0:T(8,128)(2,1)}), bf16[32,20,512]{2,1,0:T(8,128)(2,1)S(1)}, u32[]{:S(2)}, u32[]{:S(2)}) async-start(bf16[32,20,512]{2,1,0:T(8,128)(2,1)} %all_to_all.35), calls=%async_computation.2 | async-start | bytes 1572864 | tf_op jit(solution)/shard_map/all_to_all | solution.py:94
  267.5 0.1 convert_element_type.75
  267.7 0.1 copy.17
  267.8 0.2 broadcast_multiply_fusion
  268.0 1.5 fusion.12
  269.5 1.6 fusion.11
  271.1 41.0 %all-to-all-done.2 = bf16[32,20,512]{2,1,0:T(8,128)(2,1)S(1)} async-done(((bf16[32,20,512]{2,1,0:T(8,128)(2,1)}), bf16[32,20,512]{2,1,0:T(8,128)(2,1)S(1)}, u32[]{:S(2)}, u32[]{:S(2)}) %all-to-all-start.2) | async-done | bytes 655392 | tf_op jit(solution)/shard_map/all_to_all | solution.py:94
  312.1 0.1 all_to_all.37
  312.3 1.2 gather_fusion.2
  313.4 0.0 all-gather.5.cloned.1.call-done
  313.4 7.7 %fusion = bf16[256,512]{1,0:T(8,128)(2,1)} fusion(bf16[256,8192]{1,0:T(8,128)(2,1)} %all-gather.3.cloned.1.call-done, bf16[512,8192]{1,0:T(8,128)(2,1)} %all-gather.5.cloned.1.call-done, bf16[256,512]{1,0:T(8,128)(2,1)S(1)} %gather_fusion.2), kind=kOutput, calls=%fused_computation.10 | convolution fusion | flops 2147876864 | bytes 13107200 | tf_op jit(solution)/shard_map/dot_general | solution.py:21
  (11 shorter events, 0.1 us)
Async XLA Ops:
  8.0 94.1 %copy-start = (bf16[512,512]{1,0:T(8,128)(2,1)S(1)}, bf16[512,512]{1,0:T(8,128)(2,1)}, u32[]{:S(2)}) copy-start(bf16[512,512]{1,0:T(8,128)(2,1)} %param.10) | copy-start | bytes 1572868
  8.0 75.7 %all-gather.3.cloned.1.call-start = ((), (), s32[]{:S(2)}) async-start(), calls=%async_computation.4 | async-start | bytes 4456448 | tf_op jit(solution)/shard_map/all_gather | solution.py:18
  16.9 28.5 %all-to-all-start.1 = ((bf16[32,20,1]{1,2,0:T(2,128)(2,1)}), bf16[32,20,1]{1,2,0:T(2,128)(2,1)S(1)}, u32[]{:S(2)}, u32[]{:S(2)}) async-start(bf16[32,20,1]{1,2,0:T(2,128)(2,1)} %all_to_all.41), calls=%async_computation.1 | async-start | bytes 32768 | tf_op jit(solution)/shard_map/all_to_all | solution.py:52
  45.4 49.8 %all-to-all-start.3 = ((bf16[32,20,512]{2,1,0:T(8,128)(2,1)}), bf16[32,20,512]{2,1,0:T(8,128)(2,1)S(1)}, u32[]{:S(2)}, u32[]{:S(2)}) async-start(bf16[32,20,512]{2,1,0:T(8,128)(2,1)} %all_to_all.38), calls=%async_computation.3 | async-start | bytes 1572864 | tf_op jit(solution)/shard_map/all_to_all | solution.py:50
  95.2 51.1 %all-to-all-start = ((bf16[32,20,512]{2,1,0:T(8,128)(2,1)}), bf16[32,20,512]{2,1,0:T(8,128)(2,1)S(1)}, u32[]{:S(2)}, u32[]{:S(2)}) async-start(bf16[32,20,512]{2,1,0:T(8,128)(2,1)} %all_to_all.30), calls=%async_computation | async-start | bytes 1572864 | tf_op jit(solution)/shard_map/all_to_all | solution.py:51
  101.7 148.1 %all-reduce.5.cloned.1.call-start = ((), (), s32[]{:S(2)}) async-start(), calls=%async_computation.6 | async-start | bytes 163840 | tf_op jit(solution)/shard_map/psum | solution.py:75
  149.1 164.3 %all-gather.5.cloned.1.call-start = ((), (), s32[]{:S(2)}) async-start(), calls=%async_computation.5 | async-start | bytes 8650752 | tf_op jit(solution)/shard_map/all_gather | solution.py:23
  252.6 59.5 %all-to-all-start.2 = ((bf16[32,20,512]{2,1,0:T(8,128)(2,1)}), bf16[32,20,512]{2,1,0:T(8,128)(2,1)S(1)}, u32[]{:S(2)}, u32[]{:S(2)}) async-start(bf16[32,20,512]{2,1,0:T(8,128)(2,1)} %all_to_all.35), calls=%async_computation.2 | async-start | bytes 1572864 | tf_op jit(solution)/shard_map/all_to_all | solution.py:94
Sparse Core Ops, SparseCore 0:
  11.8 71.8 all-gather.2
  149.3 100.4 all-reduce.4
Sparse Core Ops, SparseCore 1:
  151.7 85.5 all-gather.4
where the time goes:
time: 329 us
  waiting for transfers between devices  232 us (71%)
  starting transfers between devices  43.5 us (13%)
  local copies, waits for them, and re-layouts  21.2 us (6%)
  between operations  15.8 us (5%)
  matrix products  13.7 us (4%)
    psum x1, waiting for transfers between devices, per_device(): lax.psum((rank_inputs, rank_gradients), 'tensor')  100 us
    all_to_all x1, waiting for transfers between devices, per_device(): lax.all_to_all(send_grads, 'adapter', split_axis=0, concat_axis=0, tiled=...  42.6 us
    all_to_all x1, waiting for transfers between devices, per_device(): lax.all_to_all(adapter_block, 'adapter', split_axis=0, concat_axis=0, til...  41 us
    all_gather x1, waiting for transfers between devices, per_device(): full_grad = lax.all_gather(output_grad, 'tensor', axis=0, tiled=True)  33.1 us
    all_to_all x1, starting transfers between devices, per_device(): lax.all_to_all(send_labels, 'adapter', split_axis=0, concat_axis=0, tiled...  16.7 us
    all_to_all x1, starting transfers between devices, per_device(): lax.all_to_all(adapter_block, 'adapter', split_axis=0, concat_axis=0, til...  14.9 us
    dot_general x1, matrix products, per_device(): lax.dot_general(full_grad, lax.all_gather(base_weight, 'adapter', axis=1,...  7.74 us
    all_to_all x1, waiting for transfers between devices, per_device(): lax.all_to_all(send_labels, 'adapter', split_axis=0, concat_axis=0, tiled...  6.95 us
  transfers between devices with their start and end apart: 7, of which 6 were waited for; matrix products, arithmetic and copies ran while one was open for 7% of the time, Pallas kernels for 0%

commit v1 on v0

v1 whole, which is shorter than its diff:
```python
import functools

import jax
import jax.numpy as jnp
from jax import lax
from jax.experimental import pallas as pl
from jax.experimental.pallas import tpu as pltpu
from jax.sharding import PartitionSpec as P

ADAPTER_RANK = 16
ADAPTER_SCALE = 2.0
MESH = pl.DeviceIdType.MESH
ANY = pl.BlockSpec(memory_space=pl.ANY)
VMEM = pl.BlockSpec(memory_space=pltpu.VMEM)
SIDE = 4
LABEL_ROWS = 16


def remote(src, dst, send_sem, recv_sem, **where):
    return pltpu.make_async_remote_copy(
        src_ref=src,
        dst_ref=dst,
        send_sem=send_sem,
        recv_sem=recv_sem,
        device_id=where,
        device_id_type=MESH,
    )


def partner(q, chips):
    me = lax.axis_index("adapter")
    z, core = me // 2, me % 2
    i, flip = q // 2, (q + 1) % 2
    half = chips // 2
    shift = half + (1 - 2 * (i % 2)) * ((i + 1) // 2)
    return ((z + shift) % chips) * 2 + (core + flip) % 2


def signal(barrier, **where):
    pl.semaphore_signal(barrier, inc=1, device_id=where, device_id_type=MESH)


def loop(n, body):
    def step(k, carry):
        body(k)
        return carry

    lax.fori_loop(0, n, step, 0)


def exchange(owners, rows, src, dst, send_sem, recv_sem):
    me = lax.axis_index("adapter")

    def copy(q):
        to = partner(q, owners // 2)
        return remote(
            src.at[pl.ds(pl.multiple_of(to * rows, rows), rows)],
            dst.at[pl.ds(pl.multiple_of(me * rows, rows), rows)],
            send_sem.at[q],
            recv_sem.at[q],
            adapter=to,
        )

    return copy


def own_block(rows, src, dst, sem):
    me = lax.axis_index("adapter")
    mine = pl.ds(pl.multiple_of(me * rows, rows), rows)
    return pltpu.make_async_copy(src.at[mine], dst.at[mine], sem)


def greet_owners(owners, barrier):
    loop(owners - 1, lambda q: signal(barrier, adapter=partner(q, owners // 2)))


def swap_kernel(owners, rows, src, dst, send_sem, recv_sem, own_sem):
    barrier = pltpu.get_barrier_semaphore()
    greet_owners(owners, barrier)
    pl.semaphore_wait(barrier, owners - 1)
    copy = exchange(owners, rows, src, dst, send_sem, recv_sem)
    loop(owners - 1, lambda q: copy(q).start())
    own = own_block(rows, src, dst, own_sem)
    own.start()
    own.wait()
    loop(owners - 1, lambda q: copy(q).wait())


def swap(slots, owners, call):
    rows = slots.shape[0] // owners
    return pl.pallas_call(
        functools.partial(swap_kernel, owners, rows),
        out_shape=jax.ShapeDtypeStruct(slots.shape, slots.dtype),
        in_specs=[VMEM],
        out_specs=ANY,
        scratch_shapes=[
            pltpu.SemaphoreType.DMA((owners,)),
            pltpu.SemaphoreType.DMA((owners,)),
            pltpu.SemaphoreType.DMA,
        ],
        compiler_params=pltpu.CompilerParams(collective_id=call, has_side_effects=True),
    )(slots)


def first_kernel(
    owners, rows, src, labels, grad, dst, labels_out, full,
    send_sem, recv_sem, label_send, label_recv, own_sem, ring_send, ring_recv,
):
    t = lax.axis_index("tensor")
    x, y = t // SIDE, t % SIDE
    tokens, width = grad.shape
    half, quarter = width // 2, width // 4

    def at(x_at, y_at):
        return (x_at % SIDE) * SIDE + y_at % SIDE

    barrier = pltpu.get_barrier_semaphore()
    greet_owners(owners, barrier)
    for dx, dy in ((1, 0), (3, 0), (0, 1), (0, 3)):
        signal(barrier, tensor=at(x + dx, y + dy))
    pl.semaphore_wait(barrier, owners + 3)

    copy = exchange(owners, rows, src, dst, send_sem, recv_sem)
    label = exchange(owners, LABEL_ROWS, labels, labels_out, label_send, label_recv)

    def cut(block, first, size):
        return full.at[pl.ds(pl.multiple_of(block * tokens, tokens), tokens), pl.ds(first, size)]

    def mine(first, size):
        return grad.at[:, pl.ds(first, size)]

    started = []

    def send(src_ref, block, first, size, sem, to):
        c = remote(src_ref, cut(block, first, size), ring_send.at[sem], ring_recv.at[sem], tensor=to)
        c.start()
        started.append(c)
        return c

    def along(side, d, e):
        return at(x + d, y + e) if side == 0 else at(x + e, y + d)

    first_hop, second = [], [[], []]
    for side in (0, 1):
        base = side * half
        first_hop.append(
            [
                send(mine(base, half), t, base, half, side * 20, along(side, 1, 0)),
                send(mine(base, half), t, base, half, side * 20 + 1, along(side, 3, 0)),
            ]
        )
    for side in (0, 1):
        base = side * half
        second[side].append(
            [
                send(mine(base, half), t, base, half, side * 20 + 4, along(side, 0, 1)),
                send(mine(base, half), t, base, half, side * 20 + 5, along(side, 0, 3)),
            ]
        )
    loop(owners - 1, lambda q: copy(q).start())
    loop(owners - 1, lambda q: label(q).start())
    own = [
        own_block(rows, src, dst, own_sem.at[0]),
        own_block(LABEL_ROWS, labels, labels_out, own_sem.at[1]),
        pltpu.make_async_copy(grad, cut(t, 0, width), own_sem.at[2]),
    ]
    for c in own:
        c.start()
    last_hop = []
    for side in (0, 1):
        base, sem = side * half, side * 20
        a, b = first_hop[side]
        a.wait_recv()
        from_a = along(side, 3, 0)
        f1 = send(cut(from_a, base, quarter), from_a, base, quarter, sem + 2, along(side, 1, 0))
        b.wait_recv()
        from_b = along(side, 1, 0)
        f2 = send(cut(from_b, base + quarter, quarter), from_b, base + quarter, quarter, sem + 3, along(side, 3, 0))
        last_hop.append((f1, f2))
        for j, block in ((1, from_a), (2, from_b)):
            second[side].append(
                [
                    send(cut(block, base, half), block, base, half, sem + 4 + 4 * j, along(side, 0, 1)),
                    send(cut(block, base, half), block, base, half, sem + 5 + 4 * j, along(side, 0, 3)),
                ]
            )
    for side in (0, 1):
        base, sem = side * half, side * 20
        for c in last_hop[side]:
            c.wait_recv()
        block = along(side, 2, 0)
        second[side].append(
            [
                send(cut(block, base, half), block, base, half, sem + 16, along(side, 0, 1)),
                send(cut(block, base, half), block, base, half, sem + 17, along(side, 0, 3)),
            ]
        )
    final = []
    for j in range(4):
        for side in (0, 1):
            base, sem = side * half, side * 20
            d = (0, 3, 1, 2)[j]
            a, b = second[side][j]
            a.wait_recv()
            block = along(side, d, 3)
            final.append(
                send(cut(block, base, quarter), block, base, quarter, sem + 6 + 4 * j, along(side, 0, 1))
            )
            b.wait_recv()
            block = along(side, d, 1)
            final.append(
                send(
                    cut(block, base + quarter, quarter), block, base + quarter, quarter,
                    sem + 7 + 4 * j, along(side, 0, 3),
                )
            )
    for c in final:
        c.wait_recv()
    for c in started:
        c.wait_send()
    for c in own:
        c.wait()
    loop(owners - 1, lambda q: copy(q).wait())
    loop(owners - 1, lambda q: label(q).wait())


def first(slots, labels, grad, owners, call):
    members = SIDE * SIDE
    tokens, width = grad.shape
    return pl.pallas_call(
        functools.partial(first_kernel, owners, slots.shape[0] // owners),
        out_shape=[
            jax.ShapeDtypeStruct(slots.shape, slots.dtype),
            jax.ShapeDtypeStruct(labels.shape, labels.dtype),
            jax.ShapeDtypeStruct((members * tokens, width), grad.dtype),
        ],
        in_specs=[VMEM] * 3,
        out_specs=[ANY] * 3,
        scratch_shapes=[
            pltpu.SemaphoreType.DMA((owners,)),
            pltpu.SemaphoreType.DMA((owners,)),
            pltpu.SemaphoreType.DMA((owners,)),
            pltpu.SemaphoreType.DMA((owners,)),
            pltpu.SemaphoreType.DMA((3,)),
            pltpu.SemaphoreType.DMA((40,)),
            pltpu.SemaphoreType.DMA((40,)),
        ],
        compiler_params=pltpu.CompilerParams(collective_id=call, has_side_effects=True),
    )(slots, labels, grad)


def weight_kernel(
    owners, members, weight, part, full, parts, ring_send, ring_recv, twin_send, twin_recv, part_send, part_recv, own_sem,
):
    chips = owners // 2
    me, t = lax.axis_index("adapter"), lax.axis_index("tensor")
    z, core = me // 2, me % 2
    depth, width = weight.shape
    rows = depth // 2
    right, left, twin = ((z + 1) % chips) * 2 + core, ((z + chips - 1) % chips) * 2 + core, z * 2 + 1 - core
    part_rows = part.shape[0]
    far = chips // 2

    barrier = pltpu.get_barrier_semaphore()
    for to in (right, left, twin):
        signal(barrier, adapter=to)
    loop(members - 1, lambda k: signal(barrier, tensor=(t + k + 1) % members))
    pl.semaphore_wait(barrier, members + 2)

    def cut(chip, h):
        column = pl.multiple_of(((chip % chips) * 2 + core) * width, width)
        return full.at[pl.ds(h * rows, rows), pl.ds(column, width)]

    def hop(s, h, way, src=None):
        chip = z + chips - s + 1 if way == 0 else z + s - 1
        return remote(
            cut(chip, h) if src is None else src,
            cut(chip, h),
            ring_send.at[s, h, way],
            ring_recv.at[s, h, way],
            adapter=right if way == 0 else left,
        )

    def pass_on(s, h, way, src=None):
        chip = z + chips - s if way == 0 else z + s
        return remote(
            cut(chip, h) if src is None else src,
            cut(chip, h),
            twin_send.at[s, h, way],
            twin_recv.at[s, h, way],
            adapter=twin,
        )

    def share(k):
        to = (t + k + 1) % members
        return remote(
            part,
            parts.at[pl.ds(pl.multiple_of(t * part_rows, part_rows), part_rows)],
            part_send.at[k],
            part_recv.at[k],
            tensor=to,
        )

    def own(h):
        return weight.at[pl.ds(h * rows, rows)]

    loop(members - 1, lambda k: share(k).start())
    for h in (0, 1):
        for way in (0, 1):
            hop(1, h, way, own(h)).start()
    for h in (0, 1):
        pass_on(0, h, 0, own(h)).start()
    keep = [
        pltpu.make_async_copy(weight, full.at[:, pl.ds(pl.multiple_of(me * width, width), width)], own_sem.at[0]),
        pltpu.make_async_copy(
            part, parts.at[pl.ds(pl.multiple_of(t * part_rows, part_rows), part_rows)], own_sem.at[1]
        ),
    ]
    for c in keep:
        c.start()

    def step(s):
        for h in (0, 1):
            for way in (0, 1):
                hop(s - 1, h, way).wait_recv()
                hop(s, h, way).start()
                pass_on(s - 1, h, way).start()

    loop(far - 2, lambda k: step(k + 2))
    for h in (0, 1):
        for way in (0, 1):
            hop(far - 1, h, way).wait_recv()
            if h == way:
                hop(far, h, way).start()
            pass_on(far - 1, h, way).start()
    for h in (0, 1):
        hop(far, h, h).wait_recv()
        pass_on(far, h, h).start()

    def finish(k):
        for h in (0, 1):
            for way in (0, 1):
                hop(k + 1, h, way).wait_send()
                pass_on(k + 1, h, way).wait()

    loop(far - 1, finish)
    for h in (0, 1):
        hop(far, h, h).wait_send()
        pass_on(far, h, h).wait()
        pass_on(0, h, 0, own(h)).wait()
    for c in keep:
        c.wait()
    loop(members - 1, lambda k: share(k).wait())


def weights(weight, part, owners, members, call):
    depth, width = weight.shape
    steps = owners // 4 + 1
    return pl.pallas_call(
        functools.partial(weight_kernel, owners, members),
        out_shape=[
            jax.ShapeDtypeStruct((depth, owners * width), weight.dtype),
            jax.ShapeDtypeStruct((members * part.shape[0], part.shape[1]), part.dtype),
        ],
        in_specs=[VMEM] * 2,
        out_specs=[ANY] * 2,
        scratch_shapes=[
            pltpu.SemaphoreType.DMA((steps, 2, 2)),
            pltpu.SemaphoreType.DMA((steps, 2, 2)),
            pltpu.SemaphoreType.DMA((steps, 2, 2)),
            pltpu.SemaphoreType.DMA((steps, 2, 2)),
            pltpu.SemaphoreType.DMA((members,)),
            pltpu.SemaphoreType.DMA((members,)),
            pltpu.SemaphoreType.DMA((2,)),
        ],
        compiler_params=pltpu.CompilerParams(collective_id=call, has_side_effects=True),
    )(weight, part)


def dot(a, b, dims):
    return lax.dot_general(a, b, (dims, ((), ())), preferred_element_type=jnp.float32)


def per_device(attn_output, output_grad, adapter_ids, base_weight, adapter_down, adapter_up):
    owners, members = lax.axis_size("adapter"), lax.axis_size("tensor")
    tok_rows, width_part = attn_output.shape
    capacity = 5 * tok_rows // (2 * owners)
    slots = owners * capacity
    per_owner = adapter_down.shape[1] // ADAPTER_RANK
    lanes = 128

    def pack(a):
        return a.reshape(slots * width_part // lanes, lanes)

    def unpack(a):
        return a.reshape(slots, width_part)

    owner_of = adapter_ids // per_owner
    local_of = adapter_ids % per_owner
    order = jnp.arange(tok_rows, dtype=jnp.int32)
    earlier = (owner_of[:, None] == owner_of[None, :]) & (order[:, None] < order[None, :])
    rank_in = jnp.sum(earlier.astype(jnp.int32), axis=0)
    slot_of = owner_of * capacity + rank_in
    place = jnp.arange(slots, dtype=jnp.int32)[:, None] == slot_of[None, :]
    place_half = place.astype(jnp.bfloat16)
    marks = jnp.sum(jnp.where(place, (local_of + 1)[None, :], 0), axis=1).reshape(owners, 1, capacity)
    marks = jnp.pad(marks.astype(jnp.bfloat16), ((0, 0), (0, LABEL_ROWS - 1), (0, lanes - capacity)))
    send_inputs = dot(place_half, attn_output, ((1,), (0,))).astype(jnp.bfloat16)
    recv_inputs, recv_marks, full_grad = first(
        pack(send_inputs), marks.reshape(owners * LABEL_ROWS, lanes), output_grad, owners, 1
    )
    recv_inputs = unpack(recv_inputs)
    recv_marks = recv_marks.reshape(owners, LABEL_ROWS, lanes)[:, 0, :capacity].reshape(1, slots)

    grad_part = lax.dynamic_slice_in_dim(full_grad, lax.axis_index("tensor") * width_part, width_part, 1)
    send_grads = dot(place_half, grad_part, ((1,), (0,))).astype(jnp.bfloat16)
    recv_grads = unpack(swap(pack(send_grads), owners, 2))

    adapter_of_row = jnp.arange(per_owner * ADAPTER_RANK, dtype=jnp.int32)[:, None] // ADAPTER_RANK
    spread = recv_marks.astype(jnp.float32) == (adapter_of_row + 1).astype(jnp.float32)

    def fold(a):
        return jnp.where(spread, a, 0.0).reshape(per_owner, ADAPTER_RANK, slots).sum(axis=0)

    low = jnp.concatenate(
        [
            fold(dot(adapter_down, recv_inputs, ((0,), (1,)))),
            fold(dot(adapter_up, recv_grads, ((1,), (1,)))),
        ],
        axis=0,
    )
    full_weight, low_parts = weights(base_weight, low, owners, members, 3)
    low = low_parts.reshape(members, 2 * ADAPTER_RANK, slots).sum(axis=0)
    low = (ADAPTER_SCALE * low).astype(jnp.bfloat16)

    def widen(a):
        return jnp.where(spread, jnp.tile(a, (per_owner, 1)), jnp.zeros((), jnp.bfloat16))

    up_wide, wide_gradient = widen(low[:ADAPTER_RANK]), widen(low[ADAPTER_RANK:])
    adapter_block = dot(wide_gradient, adapter_down, ((0,), (1,))).astype(jnp.bfloat16)
    returned = unpack(swap(pack(adapter_block), owners, 4))
    down_grad = dot(recv_inputs, wide_gradient, ((0,), (1,)))
    up_grad = dot(up_wide, recv_grads, ((1,), (0,)))
    frozen_gradient = dot(full_grad, full_weight, ((1,), (1,)))
    adapter_contribution = dot(place_half, returned, ((0,), (0,)))
    attention_output_gradient = (frozen_gradient + adapter_contribution).astype(jnp.bfloat16)
    return (attention_output_gradient, down_grad, up_grad)


def solution(mesh):
    placed = (
        P("adapter", "tensor"),
        P(("adapter", "tensor"), None),
        P("adapter"),
        P("tensor", "adapter"),
        P("tensor", "adapter"),
        P("adapter", "tensor"),
    )
    return jax.shard_map(
        per_device,
        mesh=mesh,
        in_specs=placed,
        out_specs=(P("adapter", "tensor"), P("tensor", "adapter"), P("adapter", "tensor")),
        check_vma=False,
    )
```

time: 329 us -> 221 us (0.67)
  waiting for transfers between devices: 232 us -> 0 us
  Pallas kernels: 0 us -> 191 us
  starting transfers between devices: 43.5 us -> 0 us
  between operations: 15.8 us -> 0.84 us
  local copies, waits for them, and re-layouts: 21.2 us -> 9.9 us
    pallas_call x0 -> x4, Pallas kernels: none -> 191 us  [the longest x2 78.6 us: swap(): pl.pallas_call(functools.partial(swap_kernel, owners, rows), out_shape=ja...]
    psum x1 -> x0, waiting for transfers between devices: 100 us -> none  [per_device(): lax.psum((rank_inputs, rank_gradients), 'tensor')]
    all_to_all x4 -> x0, waiting for transfers between devices: 97.3 us -> none  [the longest x1 42.6 us: per_device(): lax.all_to_all(send_grads, 'adapter', split_axis=0, concat_axis=0, tiled=...]
    all_to_all x4 -> x0, starting transfers between devices: 43.4 us -> none  [the longest x1 16.7 us: per_device(): lax.all_to_all(send_labels, 'adapter', split_axis=0, concat_axis=0, tiled...]
    all_gather x2 -> x0, waiting for transfers between devices: 33.1 us -> none  [the longest x1 33.1 us: per_device(): full_grad = lax.all_gather(output_grad, 'tensor', axis=0, tiled=True)]
    gather x4 -> x0, local copies, waits for them, and re-layouts: 11 us -> none  [the longest x1 4.3 us: per_device(): jnp.concatenate([local_of.astype(jnp.bfloat16), jnp.full((1,), -1.0, jnp....]
    reshape x2 -> x6, local copies, waits for them, and re-layouts: 1.53 us -> 7.06 us  [the longest x3 3.68 us: pack(): return a.reshape(slots * width_part // lanes, lanes)]
    all_to_all x7 -> x0, local copies, waits for them, and re-layouts: 4.19 us -> none  [the longest x2 1.19 us: per_device(): lax.all_to_all(adapter_block, 'adapter', split_axis=0, concat_axis=0, til...]
  transfers between devices with their start and end apart: 7 -> 0, of which waited for: 6 -> 0; matrix products, arithmetic and copies ran while one was open for 7% -> 0% of each run, Pallas kernels for 0% -> 0%
where the time goes in v1:
time: 221 us
  Pallas kernels  191 us (86%)
  matrix products  16.7 us (8%)
  local copies, waits for them, and re-layouts  9.9 us (4%)
  other arithmetic  2.26 us (1%)
    pallas_call x2, Pallas kernels, swap(): pl.pallas_call(functools.partial(swap_kernel, owners, rows), out_shape=ja...  78.6 us
    pallas_call x1, Pallas kernels, weights(): pl.pallas_call(functools.partial(weight_kernel, owners, members), out_sha...  57.5 us
    pallas_call x1, Pallas kernels, first(): pl.pallas_call(functools.partial(first_kernel, owners, slots.shape[0] //...  54.9 us
    dot_general x9, matrix products, dot(): lax.dot_general(a, b, (dims, ((), ())), preferred_element_type=jnp.float32)  16.7 us

profile of v1, /device:TPU:1, one launch (start us, length us, event | category | flops | bytes accessed | tf_op | source)
XLA Modules:
  0.0 220.6 jit_solution(15541959806025286762)
XLA Ops:
  0.6 0.0 copy-start
  0.6 0.7 fusion.17
  1.4 0.1 convert_reduce_fusion
  1.5 1.3 convolution_convert_fusion.1
  2.8 1.2 reshape.221.src
  4.0 0.2 select_reduce_fusion
  4.2 0.1 convert_element_type.70
  4.4 0.7 pad.4.clone
  5.0 54.9 %shard_map.85 = (bf16[2560,128]{1,0:T(8,128)(2,1)}, bf16[512,128]{1,0:T(8,128)(2,1)}, bf16[256,8192]{1,0:T(8,128)(2,1)}) custom-call(bf16[2560,128]{1,0:T(8,128)(2,1)} %reshape.221.src, bf16[512,128]{1,0:T(8,128)(2,1)} %bitcast.37, bf16[16,8192]{1,0:T(8,128)(2,1)} %grad.1), custom_call_target="tpu_custom_call" | custom-call | tf_op jit(solution)/shard_map/pallas_call | solution.py:230
  59.9 1.3 convolution_convert_fusion
  61.2 1.2 reshape.226.src
  62.5 0.0 copy-start.4
  62.5 39.5 %shard_map.86 = bf16[2560,128]{1,0:T(8,128)(2,1)} custom-call(bf16[2560,128]{1,0:T(8,128)(2,1)} %reshape.226.src), custom_call_target="tpu_custom_call" | custom-call | tf_op jit(solution)/shard_map/pallas_call | solution.py:91
  102.0 1.5 reshape.227
  103.5 0.9 slice.12
  104.3 0.1 reshape.232
  104.4 0.0 copy-done.4
  104.5 0.6 compare_select_fusion.1
  105.1 0.0 copy-start.2
  105.1 0.1 reduce_sum.48
  105.2 1.0 copy-done.2
  106.2 0.4 reshape.224
  106.5 0.0 copy-done
  106.6 0.6 compare_select_fusion.2
  107.2 0.1 reduce_sum.47
  107.3 0.6 pad_maximum_fusion.part
  107.9 57.5 %shard_map.87 = (bf16[512,8192]{1,0:T(8,128)(2,1)}, f32[512,640]{1,0:T(8,128)}) custom-call(bf16[512,256]{1,0:T(8,128)(2,1)} %weight.1, f32[32,640]{1,0:T(8,128)} %pad_maximum_fusion.part), custom_call_target="tpu_custom_call" | custom-call | tf_op jit(solution)/shard_map/pallas_call | solution.py:359
  165.4 0.0 copy-start.1
  165.4 7.9 %fusion.21 = f32[256,512]{1,0:T(8,128)} fusion(bf16[256,8192]{1,0:T(8,128)(2,1)} %get-tuple-element.8, bf16[512,8192]{1,0:T(8,128)(2,1)} %get-tuple-element.11), kind=kOutput, calls=%fused_computation.55 | convolution fusion | flops 2147483648 | bytes 13107200 | tf_op jit(solution)/shard_map/dot_general | solution.py:381
  173.3 0.0 copy-done.1
  173.3 0.1 reduce_sum.49
  173.4 0.1 tile.6
  173.5 0.7 convolution_convert_fusion.2
  174.2 1.2 reshape.230.src
  175.4 0.0 copy-start.3
  175.4 39.1 %shard_map.88 = bf16[2560,128]{1,0:T(8,128)(2,1)} custom-call(bf16[2560,128]{1,0:T(8,128)(2,1)} %reshape.230.src), custom_call_target="tpu_custom_call" | custom-call | tf_op jit(solution)/shard_map/pallas_call | solution.py:91
  214.5 1.5 reshape.231
  216.0 0.0 copy-done.3
  216.0 1.1 fusion
  217.2 0.3 compare_select_fusion.3
  217.5 1.6 fusion.22
  219.1 1.5 fusion.23
  (7 shorter events, 0.1 us)
Async XLA Ops:
  0.6 105.9 %copy-start = (bf16[512,512]{1,0:T(8,128)(2,1)S(1)}, bf16[512,512]{1,0:T(8,128)(2,1)}, u32[]{:S(2)}) copy-start(bf16[512,512]{1,0:T(8,128)(2,1)} %param.10) | copy-start | bytes 1572868
  62.5 42.0 %copy-start.4 = (bf16[512,512]{1,0:T(8,128)(2,1)S(1)}, bf16[512,512]{1,0:T(8,128)(2,1)}, u32[]{:S(2)}) copy-start(bf16[512,512]{1,0:T(8,128)(2,1)} %param.11) | copy-start | bytes 1572868
  105.1 1.1 copy-start.2
  165.4 7.9 %copy-start.1 = (f32[512,640]{1,0:T(8,128)S(1)}, f32[512,640]{1,0:T(8,128)}, u32[]{:S(2)}) copy-start(f32[512,640]{1,0:T(8,128)} %get-tuple-element.12) | copy-start | bytes 3932164
  175.4 40.6 %copy-start.3 = (f32[256,512]{1,0:T(8,128)S(1)}, f32[256,512]{1,0:T(8,128)}, u32[]{:S(2)}) copy-start(f32[256,512]{1,0:T(8,128)} %fusion.21) | copy-start | bytes 1572868

commit v2 on v1

--- a/solution.py
+++ b/solution.py
@@ -13,7 +13,6 @@
 ANY = pl.BlockSpec(memory_space=pl.ANY)
 VMEM = pl.BlockSpec(memory_space=pltpu.VMEM)
 SIDE = 4
-LABEL_ROWS = 16
 
 
 def remote(src, dst, send_sem, recv_sem, **where):
@@ -36,6 +35,10 @@
     return ((z + shift) % chips) * 2 + (core + flip) % 2
 
 
+def dot(a, b, dims):
+    return lax.dot_general(a, b, (dims, ((), ())), preferred_element_type=jnp.float32)
+
+
 def signal(barrier, **where):
     pl.semaphore_signal(barrier, inc=1, device_id=where, device_id_type=MESH)
 
@@ -74,7 +77,90 @@
     loop(owners - 1, lambda q: signal(barrier, adapter=partner(q, owners // 2)))
 
 
-def swap_kernel(owners, rows, src, dst, send_sem, recv_sem, own_sem):
+def label_kernel(
+    owners, members, rows, src, marks, dst, marks_out,
+    send_sem, recv_sem, away_send, away_recv, near_send, near_recv, own_sem,
+):
+    me, t = lax.axis_index("adapter"), lax.axis_index("tensor")
+    chips = owners // 2
+    z, core = me // 2, me % 2
+    above, below = (z + t) % chips, (z + chips - t) % chips
+    depth = marks.shape[0]
+
+    barrier = pltpu.get_barrier_semaphore()
+    greet_owners(owners, barrier)
+    loop(members - 1, lambda k: signal(barrier, tensor=(t + k + 1) % members))
+    pl.semaphore_wait(barrier, owners + members - 2)
+
+    def block(first, blocks):
+        return marks_out.at[pl.ds(pl.multiple_of(first * depth, depth), blocks * depth)]
+
+    def away(flip):
+        return remote(
+            marks, block(me, 1), away_send.at[flip], away_recv.at[flip], adapter=above * 2 + (core + flip) % 2
+        )
+
+    def near(k):
+        to = (t + k + 1) % members
+        pair = block(below * 2, 2)
+        return remote(pair, pair, near_send.at[k], near_recv.at[k], tensor=to)
+
+    keep = pltpu.make_async_copy(marks, block(me, 1), own_sem.at[1])
+
+    @pl.when(t == 0)
+    def _():
+        keep.start()
+
+    @pl.when(t > 0)
+    def _():
+        away(0).start()
+
+    away(1).start()
+    copy = exchange(owners, rows, src, dst, send_sem, recv_sem)
+    loop(owners - 1, lambda q: copy(q).start())
+    own = own_block(rows, src, dst, own_sem.at[0])
+    own.start()
+
+    @pl.when(t == 0)
+    def _():
+        keep.wait()
+
+    @pl.when(t > 0)
+    def _():
+        away(0).wait()
+
+    away(1).wait()
+    loop(members - 1, lambda k: near(k).start())
+    own.wait()
+    loop(members - 1, lambda k: near(k).wait())
+    loop(owners - 1, lambda q: copy(q).wait())
+
+
+def swap_labels(slots, marks, owners, members, call):
+    return pl.pallas_call(
+        functools.partial(label_kernel, owners, members, slots.shape[0] // owners),
+        out_shape=[
+            jax.ShapeDtypeStruct(slots.shape, slots.dtype),
+            jax.ShapeDtypeStruct((owners * marks.shape[0], marks.shape[1]), marks.dtype),
+        ],
+        in_specs=[VMEM] * 2,
+        out_specs=[ANY] * 2,
+        scratch_shapes=[
+            pltpu.SemaphoreType.DMA((owners,)),
+            pltpu.SemaphoreType.DMA((owners,)),
+            pltpu.SemaphoreType.DMA((2,)),
+            pltpu.SemaphoreType.DMA((2,)),
+            pltpu.SemaphoreType.DMA((members,)),
+            pltpu.SemaphoreType.DMA((members,)),
+            pltpu.SemaphoreType.DMA((2,)),
+        ],
+        compiler_params=pltpu.CompilerParams(collective_id=call, has_side_effects=True),
+    )(slots, marks)
+
+
+def last_kernel(
+    owners, rows, src, grad, weight, dst, product, send_sem, recv_sem, own_sem, grad_held, weight_held, load_sem,
+):
     barrier = pltpu.get_barrier_semaphore()
     greet_owners(owners, barrier)
     pl.semaphore_wait(barrier, owners - 1)
@@ -82,29 +168,60 @@
     loop(owners - 1, lambda q: copy(q).start())
     own = own_block(rows, src, dst, own_sem)
     own.start()
+    steps = load_sem.shape[0]
+    width = grad.shape[1] // steps
+
+    def part(k):
+        return pl.ds(pl.multiple_of(k * width, width), width)
+
+    def load(k):
+        return (
+            pltpu.make_async_copy(grad.at[:, part(k)], grad_held.at[:, part(k)], load_sem.at[k, 0]),
+            pltpu.make_async_copy(weight.at[:, part(k)], weight_held.at[:, part(k)], load_sem.at[k, 1]),
+        )
+
+    def fetch(k):
+        for c in load(k):
+            c.start()
+
+    def step(k):
+        for c in load(k):
+            c.wait()
+        product[...] += dot(grad_held[:, part(k)], weight_held[:, part(k)], ((1,), (1,)))
+
+    loop(steps, fetch)
+    product[...] = jnp.zeros_like(product)
+    loop(steps, step)
     own.wait()
     loop(owners - 1, lambda q: copy(q).wait())
 
 
-def swap(slots, owners, call):
-    rows = slots.shape[0] // owners
+def last(slots, grad, weight, owners, call):
+    steps = 8
     return pl.pallas_call(
-        functools.partial(swap_kernel, owners, rows),
-        out_shape=jax.ShapeDtypeStruct(slots.shape, slots.dtype),
-        in_specs=[VMEM],
-        out_specs=ANY,
+        functools.partial(last_kernel, owners, slots.shape[0] // owners),
+        out_shape=[
+            jax.ShapeDtypeStruct(slots.shape, slots.dtype),
+            jax.ShapeDtypeStruct((grad.shape[0], weight.shape[0]), jnp.float32),
+        ],
+        in_specs=[VMEM, ANY, ANY],
+        out_specs=[ANY, VMEM],
         scratch_shapes=[
             pltpu.SemaphoreType.DMA((owners,)),
             pltpu.SemaphoreType.DMA((owners,)),
             pltpu.SemaphoreType.DMA,
-        ],
-        compiler_params=pltpu.CompilerParams(collective_id=call, has_side_effects=True),
-    )(slots)
+            pltpu.VMEM(grad.shape, grad.dtype),
+            pltpu.VMEM(weight.shape, weight.dtype),
+            pltpu.SemaphoreType.DMA((steps, 2)),
+        ],
+        compiler_params=pltpu.CompilerParams(
+            collective_id=call, has_side_effects=True, vmem_limit_bytes=32 * 1024 * 1024
+        ),
+    )(slots, grad, weight)
 
 
 def first_kernel(
-    owners, rows, src, labels, grad, dst, labels_out, full,
-    send_sem, recv_sem, label_send, label_recv, own_sem, ring_send, ring_recv,
+    owners, rows, src, grad, dst, full, send_sem, recv_sem, own_sem, ring_send, ring_recv,
 ):
     t = lax.axis_index("tensor")
     x, y = t // SIDE, t % SIDE
@@ -121,7 +238,6 @@
     pl.semaphore_wait(barrier, owners + 3)
 
     copy = exchange(owners, rows, src, dst, send_sem, recv_sem)
-    label = exchange(owners, LABEL_ROWS, labels, labels_out, label_send, label_recv)
 
     def cut(block, first, size):
         return full.at[pl.ds(pl.multiple_of(block * tokens, tokens), tokens), pl.ds(first, size)]
@@ -158,11 +274,9 @@
             ]
         )
     loop(owners - 1, lambda q: copy(q).start())
-    loop(owners - 1, lambda q: label(q).start())
     own = [
         own_block(rows, src, dst, own_sem.at[0]),
-        own_block(LABEL_ROWS, labels, labels_out, own_sem.at[1]),
-        pltpu.make_async_copy(grad, cut(t, 0, width), own_sem.at[2]),
+        pltpu.make_async_copy(grad, cut(t, 0, width), own_sem.at[1]),
     ]
     for c in own:
         c.start()
@@ -221,32 +335,28 @@
     for c in own:
         c.wait()
     loop(owners - 1, lambda q: copy(q).wait())
-    loop(owners - 1, lambda q: label(q).wait())
-
-
-def first(slots, labels, grad, owners, call):
+
+
+def first(slots, grad, owners, call):
     members = SIDE * SIDE
     tokens, width = grad.shape
     return pl.pallas_call(
         functools.partial(first_kernel, owners, slots.shape[0] // owners),
         out_shape=[
             jax.ShapeDtypeStruct(slots.shape, slots.dtype),
-            jax.ShapeDtypeStruct(labels.shape, labels.dtype),
             jax.ShapeDtypeStruct((members * tokens, width), grad.dtype),
         ],
-        in_specs=[VMEM] * 3,
-        out_specs=[ANY] * 3,
+        in_specs=[VMEM] * 2,
+        out_specs=[ANY] * 2,
         scratch_shapes=[
             pltpu.SemaphoreType.DMA((owners,)),
             pltpu.SemaphoreType.DMA((owners,)),
-            pltpu.SemaphoreType.DMA((owners,)),
-            pltpu.SemaphoreType.DMA((owners,)),
-            pltpu.SemaphoreType.DMA((3,)),
+            pltpu.SemaphoreType.DMA((2,)),
             pltpu.SemaphoreType.DMA((40,)),
             pltpu.SemaphoreType.DMA((40,)),
         ],
         compiler_params=pltpu.CompilerParams(collective_id=call, has_side_effects=True),
-    )(slots, labels, grad)
+    )(slots, grad)
 
 
 def weight_kernel(
@@ -377,10 +487,6 @@
     )(weight, part)
 
 
-def dot(a, b, dims):
-    return lax.dot_general(a, b, (dims, ((), ())), preferred_element_type=jnp.float32)
-
-
 def per_device(attn_output, output_grad, adapter_ids, base_weight, adapter_down, adapter_up):
     owners, members = lax.axis_size("adapter"), lax.axis_size("tensor")
     tok_rows, width_part = attn_output.shape
@@ -403,18 +509,19 @@
     slot_of = owner_of * capacity + rank_in
     place = jnp.arange(slots, dtype=jnp.int32)[:, None] == slot_of[None, :]
     place_half = place.astype(jnp.bfloat16)
-    marks = jnp.sum(jnp.where(place, (local_of + 1)[None, :], 0), axis=1).reshape(owners, 1, capacity)
-    marks = jnp.pad(marks.astype(jnp.bfloat16), ((0, 0), (0, LABEL_ROWS - 1), (0, lanes - capacity)))
+    marks = jnp.sum(jnp.where(place, (local_of + 1)[None, :], 0), axis=1).reshape(owners, capacity)
+    marks = jnp.pad(marks.astype(jnp.bfloat16), ((0, 0), (0, lanes - capacity)))
     send_inputs = dot(place_half, attn_output, ((1,), (0,))).astype(jnp.bfloat16)
-    recv_inputs, recv_marks, full_grad = first(
-        pack(send_inputs), marks.reshape(owners * LABEL_ROWS, lanes), output_grad, owners, 1
-    )
+    recv_inputs, full_grad = first(pack(send_inputs), output_grad, owners, 1)
     recv_inputs = unpack(recv_inputs)
-    recv_marks = recv_marks.reshape(owners, LABEL_ROWS, lanes)[:, 0, :capacity].reshape(1, slots)
 
     grad_part = lax.dynamic_slice_in_dim(full_grad, lax.axis_index("tensor") * width_part, width_part, 1)
     send_grads = dot(place_half, grad_part, ((1,), (0,))).astype(jnp.bfloat16)
-    recv_grads = unpack(swap(pack(send_grads), owners, 2))
+    recv_grads, all_marks = swap_labels(pack(send_grads), marks, owners, members, 2)
+    recv_grads = unpack(recv_grads)
+    recv_marks = lax.dynamic_slice_in_dim(
+        all_marks.reshape(owners, owners, lanes), lax.axis_index("adapter"), 1, 1
+    )[:, 0, :capacity].reshape(1, slots)
 
     adapter_of_row = jnp.arange(per_owner * ADAPTER_RANK, dtype=jnp.int32)[:, None] // ADAPTER_RANK
     spread = recv_marks.astype(jnp.float32) == (adapter_of_row + 1).astype(jnp.float32)
@@ -438,10 +545,10 @@
 
     up_wide, wide_gradient = widen(low[:ADAPTER_RANK]), widen(low[ADAPTER_RANK:])
     adapter_block = dot(wide_gradient, adapter_down, ((0,), (1,))).astype(jnp.bfloat16)
-    returned = unpack(swap(pack(adapter_block), owners, 4))
+    returned, frozen_gradient = last(pack(adapter_block), full_grad, full_weight, owners, 4)
+    returned = unpack(returned)
     down_grad = dot(recv_inputs, wide_gradient, ((0,), (1,)))
     up_grad = dot(up_wide, recv_grads, ((1,), (0,)))
-    frozen_gradient = dot(full_grad, full_weight, ((1,), (1,)))
     adapter_contribution = dot(place_half, returned, ((0,), (0,)))
     attention_output_gradient = (frozen_gradient + adapter_contribution).astype(jnp.bfloat16)
     return (attention_output_gradient, down_grad, up_grad)

time: 221 us -> 212 us (0.959)
  matrix products: 16.7 us -> 8.82 us
  Pallas kernels: 191 us -> 185 us
  local copies, waits for them, and re-layouts: 9.9 us -> 13.6 us
    dot_general x9 -> x8, matrix products: 16.7 us -> 8.82 us  [dot(): lax.dot_general(a, b, (dims, ((), ())), preferred_element_type=jnp.float32)]
    pallas_call x1, Pallas kernels: 54.9 us -> 48.1 us  [first(): pl.pallas_call(functools.partial(first_kernel, owners, slots.shape[0] //...]
    unnamed x10 -> x14, local copies, waits for them, and re-layouts: 1.02 us -> 6.59 us
where the time goes in v2:
time: 212 us; the launch traced here: 211 us
  Pallas kernels  185 us (87%)
  local copies, waits for them, and re-layouts  13.6 us (6%)
  matrix products  8.82 us (4%)
  other arithmetic  3.58 us (2%)
    pallas_call x1, Pallas kernels, weights(): pl.pallas_call(functools.partial(weight_kernel, owners, members), out_sha...  58.3 us
    pallas_call x1, Pallas kernels, first(): pl.pallas_call(functools.partial(first_kernel, owners, slots.shape[0] //...  48.1 us
    pallas_call x1, Pallas kernels, swap_labels(): pl.pallas_call(functools.partial(label_kernel, owners, members, slots.sha...  40 us
    pallas_call x1, Pallas kernels, last(): pl.pallas_call(functools.partial(last_kernel, owners, slots.shape[0] // o...  38.3 us
    dot_general x8, matrix products, dot(): lax.dot_general(a, b, (dims, ((), ())), preferred_element_type=jnp.float32)  8.82 us
    unnamed x14, local copies, waits for them, and re-layouts  6.59 us

profile of v2, /device:TPU:1, one launch (start us, length us, event | category | flops | bytes accessed | tf_op | source)
XLA Modules:
  0.0 211.5 jit_solution(11382937821917883348)
XLA Ops:
  0.6 0.0 copy-start
  0.6 0.7 fusion.17
  1.4 0.1 convert_reduce_fusion
  1.5 1.3 convolution_convert_fusion.1
  2.8 1.2 reshape.206.src
  4.0 48.1 %shard_map.85 = (bf16[2560,128]{1,0:T(8,128)(2,1)}, bf16[256,8192]{1,0:T(8,128)(2,1)}) custom-call(bf16[2560,128]{1,0:T(8,128)(2,1)} %reshape.206.src, bf16[16,8192]{1,0:T(8,128)(2,1)} %grad.1), custom_call_target="tpu_custom_call" | custom-call | tf_op jit(solution)/shard_map/pallas_call | solution.py:343
  52.2 1.3 convolution_convert_fusion
  53.5 1.2 reshape.207.src
  54.7 0.0 copy-start.6
  54.7 0.2 select_reduce_fusion
  54.9 0.1 convert_element_type.53
  55.0 0.6 pad.4.marks
  55.6 40.0 %shard_map.86 = (bf16[2560,128]{1,0:T(8,128)(2,1)}, bf16[1024,128]{1,0:T(8,128)(2,1)}) custom-call(bf16[2560,128]{1,0:T(8,128)(2,1)} %reshape.207.src, bf16[32,128]{1,0:T(8,128)(2,1)} %pad.4.marks), custom_call_target="tpu_custom_call" | custom-call | tf_op jit(solution)/shard_map/pallas_call | solution.py:140
  95.6 1.5 reshape.211
  97.1 0.0 copy-start.3
  97.1 1.0 constant_dynamic-slice_fusion
  98.1 0.1 reshape.216
  98.2 0.0 copy-done.6
  98.2 0.6 compare_select_fusion.1
  98.8 0.0 copy-done.3
  98.8 0.0 copy-start.5
  98.8 0.1 reduce_sum.48
  98.9 1.0 copy-done.5
  99.9 0.4 reshape.209
  100.3 0.0 copy-done
  100.3 0.6 compare_select_fusion.2
  101.0 0.1 reduce_sum.47
  101.0 0.6 pad_maximum_fusion.part
  101.7 58.3 %shard_map.87 = (bf16[512,8192]{1,0:T(8,128)(2,1)}, f32[512,640]{1,0:T(8,128)}) custom-call(bf16[512,256]{1,0:T(8,128)(2,1)} %weight.1, f32[32,640]{1,0:T(8,128)} %pad_maximum_fusion.part), custom_call_target="tpu_custom_call" | custom-call | tf_op jit(solution)/shard_map/pallas_call | solution.py:469
  160.0 1.4 reduce_sum.49
  161.4 0.1 tile.6
  161.4 0.7 convolution_convert_fusion.2
  162.2 0.4 reshape.214.src
  162.6 0.0 copy-start.1
  162.6 3.4 %copy-done.1 = bf16[512,8192]{1,0:T(8,128)(2,1)S(1)} copy-done((bf16[512,8192]{1,0:T(8,128)(2,1)S(1)}, bf16[512,8192]{1,0:T(8,128)(2,1)}, u32[]{:S(2)}) %copy-start.1) | copy-done | bytes 8388632
  166.0 0.0 copy-start.2
  166.0 2.2 %copy-done.2 = bf16[256,8192]{1,0:T(8,128)(2,1)S(1)} copy-done((bf16[256,8192]{1,0:T(8,128)(2,1)S(1)}, bf16[256,8192]{1,0:T(8,128)(2,1)}, u32[]{:S(2)}) %copy-start.2) | copy-done | bytes 4194328
  168.1 38.3 %shard_map.88 = (bf16[2560,128]{1,0:T(8,128)(2,1)S(1)}, f32[256,512]{1,0:T(8,128)S(1)}) custom-call(bf16[2560,128]{1,0:T(8,128)(2,1)S(1)} %reshape.214.src, bf16[256,8192]{1,0:T(8,128)(2,1)S(1)} %copy-done.2, bf16[512,8192]{1,0:T(8,128)(2,1)S(1)} %copy-done.1), custom_call_target="tpu_custom_call" | custom-call | tf_op jit(solution)/shard_map/pallas_call | solution.py:201
  206.5 0.4 reshape.215
  206.9 1.1 fusion
  208.0 0.3 compare_select_fusion.3
  208.3 0.0 copy-start.4
  208.3 1.6 fusion.21
  209.9 0.0 copy-done.4
  209.9 1.5 fusion.22
  (7 shorter events, 0.1 us)
Async XLA Ops:
  0.6 99.7 %copy-start = (bf16[512,512]{1,0:T(8,128)(2,1)S(1)}, bf16[512,512]{1,0:T(8,128)(2,1)}, u32[]{:S(2)}) copy-start(bf16[512,512]{1,0:T(8,128)(2,1)} %param.10) | copy-start | bytes 1572868
  54.7 43.5 %copy-start.6 = (bf16[512,512]{1,0:T(8,128)(2,1)S(1)}, bf16[512,512]{1,0:T(8,128)(2,1)}, u32[]{:S(2)}) copy-start(bf16[512,512]{1,0:T(8,128)(2,1)} %param.11) | copy-start | bytes 1572868
  97.1 1.7 copy-start.3
  98.8 1.1 copy-start.5
  162.6 3.4 %copy-start.1 = (bf16[512,8192]{1,0:T(8,128)(2,1)S(1)}, bf16[512,8192]{1,0:T(8,128)(2,1)}, u32[]{:S(2)}) copy-start(bf16[512,8192]{1,0:T(8,128)(2,1)} %get-tuple-element.16.weight) | copy-start | bytes 25165828
  166.0 2.2 %copy-start.2 = (bf16[256,8192]{1,0:T(8,128)(2,1)S(1)}, bf16[256,8192]{1,0:T(8,128)(2,1)}, u32[]{:S(2)}) copy-start(bf16[256,8192]{1,0:T(8,128)(2,1)} %get-tuple-element.11.grad) | copy-start | bytes 12582916
  208.3 1.6 copy-start.4

commit v3 on v2

--- a/solution.py
+++ b/solution.py
@@ -215,7 +215,7 @@
             pltpu.SemaphoreType.DMA((steps, 2)),
         ],
         compiler_params=pltpu.CompilerParams(
-            collective_id=call, has_side_effects=True, vmem_limit_bytes=32 * 1024 * 1024
+            collective_id=call, has_side_effects=True, vmem_limit_bytes=63 * 1024 * 1024
         ),
     )(slots, grad, weight)
 

time: 212 us -> 211 us (level)
  local copies, waits for them, and re-layouts: 13.6 us -> 10.1 us
    unnamed x14 -> x16, local copies, waits for them, and re-layouts: 6.59 us -> 1.16 us
where the time goes in v3:
time: 211 us; the launch traced here: 210 us
  Pallas kernels  187 us (89%)
  local copies, waits for them, and re-layouts  10.1 us (5%)
  matrix products  8.81 us (4%)
  other arithmetic  3.58 us (2%)
    pallas_call x1, Pallas kernels, weights(): pl.pallas_call(functools.partial(weight_kernel, owners, members), out_sha...  58.3 us
    pallas_call x1, Pallas kernels, first(): pl.pallas_call(functools.partial(first_kernel, owners, slots.shape[0] //...  48.1 us
    pallas_call x1, Pallas kernels, last(): pl.pallas_call(functools.partial(last_kernel, owners, slots.shape[0] // o...  40.3 us
    pallas_call x1, Pallas kernels, swap_labels(): pl.pallas_call(functools.partial(label_kernel, owners, members, slots.sha...  40 us
    dot_general x8, matrix products, dot(): lax.dot_general(a, b, (dims, ((), ())), preferred_element_type=jnp.float32)  8.81 us

profile of v3, /device:TPU:1, one launch (start us, length us, event | category | flops | bytes accessed | tf_op | source)
XLA Modules:
  0.0 210.1 jit_solution(7565269591651777755)
XLA Ops:
  0.6 0.0 copy-start
  0.6 0.7 fusion.17
  1.4 0.1 convert_reduce_fusion
  1.5 1.3 convolution_convert_fusion.1
  2.8 1.2 reshape.206.src
  4.0 48.1 %shard_map.85 = (bf16[2560,128]{1,0:T(8,128)(2,1)}, bf16[256,8192]{1,0:T(8,128)(2,1)}) custom-call(bf16[2560,128]{1,0:T(8,128)(2,1)} %reshape.206.src, bf16[16,8192]{1,0:T(8,128)(2,1)} %grad.1), custom_call_target="tpu_custom_call" | custom-call | tf_op jit(solution)/shard_map/pallas_call | solution.py:343
  52.2 1.3 convolution_convert_fusion
  53.5 1.2 reshape.207.src
  54.7 0.0 copy-start.7
  54.7 0.2 select_reduce_fusion
  54.9 0.1 convert_element_type.53
  55.0 0.6 pad.4.marks
  55.6 40.0 %shard_map.86 = (bf16[2560,128]{1,0:T(8,128)(2,1)}, bf16[1024,128]{1,0:T(8,128)(2,1)}) custom-call(bf16[2560,128]{1,0:T(8,128)(2,1)} %reshape.207.src, bf16[32,128]{1,0:T(8,128)(2,1)} %pad.4.marks), custom_call_target="tpu_custom_call" | custom-call | tf_op jit(solution)/shard_map/pallas_call | solution.py:140
  95.6 1.5 reshape.211
  97.1 0.0 copy-start.3
  97.1 1.0 constant_dynamic-slice_fusion
  98.1 0.1 reshape.216
  98.2 0.0 copy-done.7
  98.2 0.6 compare_select_fusion.1
  98.8 0.0 copy-done.3
  98.8 0.0 copy-start.5
  98.8 0.1 reduce_sum.48
  98.9 1.0 copy-done.5
  99.9 0.4 reshape.209
  100.3 0.0 copy-done
  100.3 0.0 copy-start.1
  100.3 0.6 compare_select_fusion.2
  101.0 0.1 reduce_sum.47
  101.0 0.1 copy-done.1
  101.2 0.6 pad_maximum_fusion.part
  101.8 58.3 %shard_map.87 = (bf16[512,8192]{1,0:T(8,128)(2,1)}, f32[512,640]{1,0:T(8,128)}) custom-call(bf16[512,256]{1,0:T(8,128)(2,1)} %weight.1, f32[32,640]{1,0:T(8,128)} %pad_maximum_fusion.part), custom_call_target="tpu_custom_call" | custom-call | tf_op jit(solution)/shard_map/pallas_call | solution.py:469
  160.1 1.4 reduce_sum.49
  161.5 0.1 tile.6
  161.6 0.7 convolution_convert_fusion.2
  162.3 1.2 reshape.214.src
  163.5 40.3 %shard_map.88 = (bf16[2560,128]{1,0:T(8,128)(2,1)}, f32[256,512]{1,0:T(8,128)}) custom-call(bf16[2560,128]{1,0:T(8,128)(2,1)} %reshape.214.src, bf16[256,8192]{1,0:T(8,128)(2,1)} %get-tuple-element.11.grad, bf16[512,8192]{1,0:T(8,128)(2,1)} %get-tuple-element.16.weight), custom_call_target="tpu_custom_call" | custom-call | tf_op jit(solution)/shard_map/pallas_call | solution.py:201
  203.9 0.0 copy-start.6
  203.9 1.5 reshape.215
  205.4 0.0 copy-done.6
  205.4 0.0 copy-start.2
  205.5 1.1 fusion
  206.6 0.3 compare_select_fusion.3
  206.9 0.0 copy-start.4
  206.9 0.0 copy-done.2
  206.9 1.6 fusion.21
  208.5 0.0 copy-done.4
  208.5 1.5 fusion.22
  (7 shorter events, 0.1 us)
Async XLA Ops:
  0.6 99.7 %copy-start = (bf16[512,512]{1,0:T(8,128)(2,1)S(1)}, bf16[512,512]{1,0:T(8,128)(2,1)}, u32[]{:S(2)}) copy-start(bf16[512,512]{1,0:T(8,128)(2,1)} %param.10) | copy-start | bytes 1572868
  54.7 43.5 %copy-start.7 = (bf16[512,512]{1,0:T(8,128)(2,1)S(1)}, bf16[512,512]{1,0:T(8,128)(2,1)}, u32[]{:S(2)}) copy-start(bf16[512,512]{1,0:T(8,128)(2,1)} %param.11) | copy-start | bytes 1572868
  97.1 1.7 copy-start.3
  98.8 1.1 copy-start.5
  100.3 0.8 copy-start.1
  203.9 1.6 copy-start.6
  205.4 1.5 copy-start.2
  206.9 1.6 copy-start.4

commit v4 on v3

--- a/solution.py
+++ b/solution.py
@@ -215,7 +215,7 @@
             pltpu.SemaphoreType.DMA((steps, 2)),
         ],
         compiler_params=pltpu.CompilerParams(
-            collective_id=call, has_side_effects=True, vmem_limit_bytes=63 * 1024 * 1024
+            collective_id=call, has_side_effects=True, vmem_limit_bytes=121 * 512 * 1024
         ),
     )(slots, grad, weight)
 

time: 211 us -> 210 us (level)
  no operation moved by 1% of the time
where the time goes in v4:
time: 210 us
  Pallas kernels  187 us (89%)
  local copies, waits for them, and re-layouts  9.88 us (5%)
  matrix products  8.82 us (4%)
  other arithmetic  3.58 us (2%)
    pallas_call x1, Pallas kernels, weights(): pl.pallas_call(functools.partial(weight_kernel, owners, members), out_sha...  58.3 us
    pallas_call x1, Pallas kernels, first(): pl.pallas_call(functools.partial(first_kernel, owners, slots.shape[0] //...  48.1 us
    pallas_call x1, Pallas kernels, last(): pl.pallas_call(functools.partial(last_kernel, owners, slots.shape[0] // o...  40.3 us
    pallas_call x1, Pallas kernels, swap_labels(): pl.pallas_call(functools.partial(label_kernel, owners, members, slots.sha...  40 us
    dot_general x8, matrix products, dot(): lax.dot_general(a, b, (dims, ((), ())), preferred_element_type=jnp.float32)  8.82 us

profile of v4, /device:TPU:1, one launch (start us, length us, event | category | flops | bytes accessed | tf_op | source)
XLA Modules:
  0.0 209.8 jit_solution(14376004679234281168)
XLA Ops:
  0.6 0.0 copy-start
  0.6 0.7 fusion.17
  1.4 0.1 convert_reduce_fusion
  1.5 1.3 convolution_convert_fusion.1
  2.8 1.2 reshape.206.src
  4.0 48.1 %shard_map.85 = (bf16[2560,128]{1,0:T(8,128)(2,1)}, bf16[256,8192]{1,0:T(8,128)(2,1)}) custom-call(bf16[2560,128]{1,0:T(8,128)(2,1)} %reshape.206.src, bf16[16,8192]{1,0:T(8,128)(2,1)} %grad.1), custom_call_target="tpu_custom_call" | custom-call | tf_op jit(solution)/shard_map/pallas_call | solution.py:343
  52.2 1.3 convolution_convert_fusion
  53.5 1.2 reshape.207.src
  54.7 0.0 copy-start.3
  54.7 0.2 select_reduce_fusion
  54.9 0.1 convert_element_type.53
  55.0 0.6 pad.4.marks
  55.6 40.0 %shard_map.86 = (bf16[2560,128]{1,0:T(8,128)(2,1)}, bf16[1024,128]{1,0:T(8,128)(2,1)}) custom-call(bf16[2560,128]{1,0:T(8,128)(2,1)} %reshape.207.src, bf16[32,128]{1,0:T(8,128)(2,1)} %pad.4.marks), custom_call_target="tpu_custom_call" | custom-call | tf_op jit(solution)/shard_map/pallas_call | solution.py:140
  95.6 1.5 reshape.211
  97.1 0.9 constant_dynamic-slice_fusion
  98.0 0.1 reshape.216
  98.1 0.0 copy-done.3
  98.1 0.6 compare_select_fusion.1
  98.7 0.0 copy-start.1
  98.7 0.1 reduce_sum.48
  98.8 1.0 copy-done.1
  99.8 0.4 reshape.209
  100.2 0.0 copy-done
  100.2 0.6 compare_select_fusion.2
  100.8 0.1 reduce_sum.47
  100.9 0.6 pad_maximum_fusion.part
  101.6 58.3 %shard_map.87 = (bf16[512,8192]{1,0:T(8,128)(2,1)}, f32[512,640]{1,0:T(8,128)}) custom-call(bf16[512,256]{1,0:T(8,128)(2,1)} %weight.1, f32[32,640]{1,0:T(8,128)} %pad_maximum_fusion.part), custom_call_target="tpu_custom_call" | custom-call | tf_op jit(solution)/shard_map/pallas_call | solution.py:469
  159.8 1.4 reduce_sum.49
  161.3 0.1 tile.6
  161.3 0.7 convolution_convert_fusion.2
  162.1 1.2 reshape.214.src
  163.3 40.3 %shard_map.88 = (bf16[2560,128]{1,0:T(8,128)(2,1)}, f32[256,512]{1,0:T(8,128)}) custom-call(bf16[2560,128]{1,0:T(8,128)(2,1)} %reshape.214.src, bf16[256,8192]{1,0:T(8,128)(2,1)} %get-tuple-element.11.grad, bf16[512,8192]{1,0:T(8,128)(2,1)} %get-tuple-element.16.weight), custom_call_target="tpu_custom_call" | custom-call | tf_op jit(solution)/shard_map/pallas_call | solution.py:201
  203.6 0.0 copy-start.2
  203.6 1.5 reshape.215
  205.2 0.0 copy-done.2
  205.2 1.1 fusion
  206.4 0.3 compare_select_fusion.3
  206.7 1.6 fusion.21
  208.3 1.5 fusion.22
  (7 shorter events, 0.1 us)
Async XLA Ops:
  0.6 99.6 %copy-start = (bf16[512,512]{1,0:T(8,128)(2,1)S(1)}, bf16[512,512]{1,0:T(8,128)(2,1)}, u32[]{:S(2)}) copy-start(bf16[512,512]{1,0:T(8,128)(2,1)} %param.10) | copy-start | bytes 1572868
  54.7 43.4 %copy-start.3 = (bf16[512,512]{1,0:T(8,128)(2,1)S(1)}, bf16[512,512]{1,0:T(8,128)(2,1)}, u32[]{:S(2)}) copy-start(bf16[512,512]{1,0:T(8,128)(2,1)} %param.11) | copy-start | bytes 1572868
  98.7 1.1 copy-start.1
  203.6 1.6 copy-start.2
